TPU v7x, 512 devices: a whole 4x8x8 slice. The times are simulated.
512 devices in a mesh: pool: 32 (over z_hi, y), ctx: 4 (over x), head: 4 (over z_lo, core).
Axes of the slice: x: 4, y: 8, z: 8 (z_hi: 4, z_lo: 2; z = z_hi * 2 + z_lo), core: 2. Of those that a mesh axis runs over, the one named last changes fastest.
Arguments:
- kv_pool: bfloat16 [4, 1024, 2, 32, 1024], P('ctx', 'pool', None, None, 'head'), may hold values from -6 to 6
- state_pool: bfloat16 [1024, 64, 1024], P('pool', 'ctx', 'head'), may hold values from -0.59765625 to 0.59765625
- block_owner: int32 [4, 1024], P('ctx'), may hold values from 0 to 31, as said below
- block_index: int32 [4, 1024], P('ctx'), may hold values from 0 to 31, as said below
- history_len: int32 [32], P('pool'), may hold values from 1 to 4096, as said below
- turn_len: int32 [32], P('pool'), may hold values from 256 to 512, as said below
- mixer_in: bfloat16 [32, 128, 64, 512], P('pool', 'head', 'ctx'), may hold values from -6 to 6
- input_proj: bfloat16 [32, 8, 256, 512], P('pool', 'head'), may hold values from -1.5 to 1.5
- output_proj: bfloat16 [32, 8, 256, 512], P('pool', 'head'), may hold values from -6 to 6
- step_size: float32 [32, 128, 512], P('pool', 'head'), may hold values from 0 to 2, as said below
- decay_rate: float32 [128], P('head'), may hold values from 0 to 4, as said below
- bypass_factor: float32 [128], P('head'), may hold values from 0.5 to 1.5
- queries: bfloat16 [32, 512, 8192], P('pool', 'ctx', 'head'), may hold values from -300 to 300
- turn_kv: bfloat16 [32, 2, 512, 1024], P('pool', None, 'ctx', 'head'), may hold values from -6 to 6
Outputs:
- mixer_out: bfloat16 [32, 128, 64, 512], P('pool', 'head', 'ctx')
- next_state: float32 [32, 128, 64, 256], P('pool', 'head', 'ctx')
- attn_out: bfloat16 [32, 512, 8192], P('pool', 'ctx', 'head')
Inputs may be any that keep to these rules, and one draw needn't show every extreme that they name: `block_owner`: in each row c, every session owns exactly 32 slots, and each aligned run of 32 slots (one pool shard) holds at most 2 blocks of any one session; in every row some shard holds exactly 2 blocks of some session. `block_index`: in each row, the slots of one session carry the indices 0 to 31, each once. `history_len`: some session has exactly 4096. `turn_len`: every value is at least 256 and some session has exactly 512. `step_size`: Positive. `decay_rate`: Positive.
All inputs are finite; a program needn't handle non-finite values.
Results may differ from a plain program's by a relative error of at most 0.008.
Values may be sent and summed in bfloat16 or wider, within the bound.
A program may use at most 64 MiB of HBM per device.

v0:
```python
import jax
import jax.numpy as jnp
from jax import lax
from jax.sharding import PartitionSpec as P

Q_HEADS = 64
KV_HEADS = 8
HEAD_DIM = 128
PAGE = 32
BLK = 128
floor_score = -1e30


def spanned_ssd(
    values, input_proj, output_proj, step_sizes, rates, bypass_factor, start_state, valid_len
):
    heads, channels, total = values.shape
    groups = input_proj.shape[0]
    per_group = heads // groups
    count = total // BLK
    positions = jnp.arange(total, dtype=jnp.int32)
    live = positions < valid_len
    step_sizes = jnp.where(live[None, :], step_sizes, jnp.float32(0.0))
    value_blocks = values.reshape(heads, channels, count, BLK).transpose(2, 0, 1, 3)
    input_blocks = input_proj.reshape(groups, -1, count, BLK).transpose(2, 0, 1, 3)
    output_blocks = output_proj.reshape(groups, -1, count, BLK).transpose(2, 0, 1, 3)
    step_blocks = step_sizes.reshape(heads, count, BLK).transpose(1, 0, 2)
    offsets = jnp.arange(BLK, dtype=jnp.int32)
    lower = offsets[:, None] >= offsets[None, :]
    exact = lax.Precision.HIGHEST

    def advance(carried, item):
        value_blk, input_blk, output_blk, step_blk = item
        value_blk = value_blk.astype(jnp.float32)
        input_blk = input_blk.astype(jnp.float32)
        output_blk = output_blk.astype(jnp.float32)
        running = jnp.cumsum(-rates[:, None] * step_blk, axis=1)
        pairs = jnp.einsum("gnt,gns->gts", output_blk, input_blk, precision=exact)
        pairs = jnp.repeat(pairs, per_group, axis=0)
        gaps = jnp.minimum(running[:, :, None] - running[:, None, :], 0.0)
        mixing = jnp.where(lower[None], jnp.exp(gaps), 0.0) * pairs * step_blk[:, None, :]
        result = jnp.einsum("hts,hps->hpt", mixing, value_blk, precision=exact)
        read_out = jnp.repeat(output_blk, per_group, axis=0)
        result = result + jnp.exp(running)[:, None, :] * jnp.einsum(
            "hpn,hnt->hpt", carried, read_out, precision=exact
        )
        result = result + bypass_factor[:, None, None] * value_blk
        weights = jnp.exp(running[:, -1:] - running) * step_blk
        write_in = jnp.repeat(input_blk, per_group, axis=0)
        carried = jnp.exp(running[:, -1])[:, None, None] * carried + jnp.einsum(
            "hps,hns->hpn", value_blk * weights[:, None, :], write_in, precision=exact
        )
        return (carried, result)

    final_state, results = lax.scan(
        advance, start_state, (value_blocks, input_blocks, output_blocks, step_blocks)
    )
    results = results.transpose(1, 2, 0, 3).reshape(heads, channels, total)
    return (jnp.where(live[None, None, :], results, 0.0), final_state)


def route_blocks(kv_local, state_local, owner_row, index_row):
    parties = lax.axis_size("pool")
    myself = lax.axis_index("pool")
    pages = kv_local.shape[1]
    capacity = 2 * pages // parties
    sessions = jnp.arange(parties, dtype=jnp.int32)
    table = (
        (owner_row[:, None] == sessions[None, :]).astype(jnp.int32).reshape(parties, pages, parties)
    )
    before = jnp.cumsum(table, axis=1) - table
    ranks = jnp.sum(before * table, axis=2)
    owners = owner_row.reshape(parties, pages)
    my_owner = lax.dynamic_index_in_dim(owners, myself, 0, keepdims=False)
    device_rank = lax.dynamic_index_in_dim(ranks, myself, 0, keepdims=False)
    send_kv = (
        jnp.zeros((parties, capacity) + kv_local.shape[2:], kv_local.dtype)
        .at[my_owner, device_rank]
        .set(kv_local[0])
    )
    send_state = (
        jnp.zeros((parties, capacity) + state_local.shape[1:], state_local.dtype)
        .at[my_owner, device_rank]
        .set(state_local)
    )
    recv_kv, recv_state = (
        lax.all_to_all(send_kv, "pool", split_axis=0, concat_axis=0, tiled=True),
        lax.all_to_all(send_state, "pool", split_axis=0, concat_axis=0, tiled=True),
    )
    flat_place = (sessions[:, None] * capacity + ranks).reshape(-1)
    target = jnp.where(owner_row == myself, index_row, pages)
    where_from = jnp.zeros((pages,), jnp.int32).at[target].set(flat_place, mode="drop")
    hist_pages = recv_kv.reshape((parties * capacity,) + recv_kv.shape[2:])[where_from]
    start_slabs = recv_state.reshape((parties * capacity,) + recv_state.shape[2:])[where_from]
    return (hist_pages, start_slabs)


def attend_block(carried, query_rows, query_index, block, seg_id, hist_rows, history_len):
    rows = query_rows.shape[0]
    key_rows = block.shape[1]
    width = block.shape[2]
    groups = width // HEAD_DIM
    per_group = Q_HEADS // KV_HEADS
    turn_rows = key_rows - hist_rows
    offsets = jnp.arange(key_rows, dtype=jnp.int32)
    in_history = offsets < hist_rows
    placed = jnp.where(
        in_history, seg_id * hist_rows + offsets, seg_id * turn_rows + offsets - hist_rows
    )
    seen_mask = jnp.where(
        in_history[None, :],
        (placed < history_len)[None, :],
        placed[None, :] <= query_index[:, None],
    )
    score_scale = HEAD_DIM ** (-0.5)
    peak, totals, summed = carried
    query_heads = query_rows.reshape(rows, groups, per_group, HEAD_DIM)
    key_heads = block[0].reshape(key_rows, groups, HEAD_DIM)
    value_heads = block[1].reshape(key_rows, groups, HEAD_DIM)
    scores = (
        jnp.einsum("rgqd,kgd->rgqk", query_heads, key_heads, preferred_element_type=jnp.float32)
        * score_scale
    )
    mask = seen_mask[:, None, None, :]
    fresh = jnp.maximum(peak, jnp.max(jnp.where(mask, scores, floor_score), axis=-1))
    weights = jnp.where(mask, jnp.exp(scores - fresh[..., None]), 0.0)
    fade = jnp.exp(peak - fresh)
    totals = fade * totals + jnp.sum(weights, axis=-1)
    summed = fade[..., None] * summed + jnp.einsum(
        "rgqk,kgd->rgqd",
        weights.astype(jnp.bfloat16),
        value_heads,
        preferred_element_type=jnp.float32,
    )
    return (fresh, totals, summed)


def context_attention(query_rows, history, turn_keys, history_len, turn_len):
    turn_rows = query_rows.shape[0]
    hist_rows = history.shape[1]
    seg_rows = hist_rows + turn_rows
    width = history.shape[-1]
    groups = width // HEAD_DIM
    per_group = Q_HEADS // KV_HEADS
    segment = lax.axis_index("ctx")
    local_keys = jnp.concatenate([history, turn_keys], axis=1)
    row_ids = jnp.arange(turn_rows, dtype=jnp.int32)
    own_index = segment * turn_rows + row_ids
    carried = (
        jnp.full((turn_rows, groups, per_group), floor_score, jnp.float32),
        jnp.zeros((turn_rows, groups, per_group), jnp.float32),
        jnp.zeros((turn_rows, groups, per_group, HEAD_DIM), jnp.float32),
    )
    piece = lax.all_gather(local_keys, "ctx", axis=1, tiled=True)
    count = piece.shape[1] // seg_rows
    blocks = piece.reshape(2, count, seg_rows, width).transpose(1, 0, 2, 3)

    def visit(inner, item):
        block, offset = item
        return (
            attend_block(inner, query_rows, own_index, block, offset, hist_rows, history_len),
            None,
        )

    carried, _ = lax.scan(visit, carried, (blocks, jnp.arange(count, dtype=jnp.int32)))
    peak, totals, summed = carried
    result = (summed / totals[..., None]).reshape(turn_rows, groups * per_group * HEAD_DIM)
    return jnp.where((own_index < turn_len)[:, None], result, 0.0).astype(jnp.bfloat16)


def local(
    kv_pool,
    state_pool,
    block_owner,
    block_index,
    history_len,
    turn_len,
    mixer_in,
    input_proj,
    output_proj,
    step_size,
    decay_rate,
    bypass_factor,
    queries,
    turn_kv,
):
    hist_pages, start_slabs = route_blocks(kv_pool, state_pool, block_owner[0], block_index[0])
    pages = hist_pages.shape[0]
    width = hist_pages.shape[-1]
    history = hist_pages.transpose(1, 0, 2, 3).reshape(2, pages * PAGE, width)
    mixed, final = spanned_ssd(
        mixer_in[0],
        input_proj[0],
        output_proj[0],
        step_size[0],
        decay_rate,
        bypass_factor,
        start_slabs.astype(jnp.float32),
        turn_len[0],
    )
    attended = context_attention(queries[0], history, turn_kv[0], history_len[0], turn_len[0])
    return (mixed.astype(jnp.bfloat16)[None], final[None], attended[None])


def solution(mesh):
    return jax.shard_map(
        local,
        mesh=mesh,
        in_specs=(
            P("ctx", "pool", None, None, "head"),
            P("pool", "ctx", "head"),
            P("ctx", None),
            P("ctx", None),
            P("pool"),
            P("pool"),
            P("pool", "head", "ctx", None),
            P("pool", "head", None, None),
            P("pool", "head", None, None),
            P("pool", "head", None),
            P("head"),
            P("head"),
            P("pool", "ctx", "head"),
            P("pool", None, "ctx", "head"),
        ),
        out_specs=(
            P("pool", "head", "ctx", None),
            P("pool", "head", "ctx", None),
            P("pool", "ctx", "head"),
        ),
        check_vma=False,
    )
```

profile of v0, /device:TPU:1, one launch (start us, length us, event | category | flops | bytes accessed | tf_op | source)
XLA Modules:
  0.0 286.1 jit_solution(10285035328454896795)
XLA Ops:
  7.7 1.3 reduce.7
  11.3 4.3 %scatter_fusion = bf16[32,2,16,256]{3,2,1,0:T(8,128)(2,1)} fusion(bf16[32,2,16,256]{3,2,1,0:T(8,128)(2,1)} %broadcast_in_dim.176, s32[32]{0:T(128)S(1)} %fusion.47, bf16[32,16,256]{2,1,0:T(8,128)(2,1)} %param.19), kind=kCustom, calls=%fused_computation.2 | custom fusion | bytes 786688 | tf_op jit(solution)/shard_map/scatter | solution.py:84
  15.6 16.5 %all-to-all-start = ((bf16[32,2,16,256]{3,2,1,0:T(8,128)(2,1)}), bf16[32,2,16,256]{3,2,1,0:T(8,128)(2,1)S(1)}, u32[]{:S(2)}, u32[]{:S(2)}) async-start(bf16[32,2,16,256]{3,2,1,0:T(8,128)(2,1)} %scatter_fusion), calls=%async_computation | async-start | bytes 1048576 | tf_op jit(solution)/shard_map/all_to_all | solution.py:88
  32.1 1.6 broadcast_in_dim.189
  33.7 5.0 %scatter_fusion.1 = bf16[32,2,2,32,256]{4,3,2,1,0:T(8,128)(2,1)} fusion(bf16[32,2,2,32,256]{4,3,2,1,0:T(8,128)(2,1)} %broadcast_in_dim.189, s32[32]{0:T(128)S(1)} %fusion.47, bf16[32,2,32,256]{3,2,1,0:T(8,128)(2,1)S(1)} %bitcast.210), kind=kCustom, calls=%fused_computation.4 | custom fusion | bytes 3145984 | tf_op jit(solution)/shard_map/scatter | solution.py:79
  38.7 9.7 %all-to-all-done = bf16[32,2,16,256]{3,2,1,0:T(8,128)(2,1)S(1)} async-done(((bf16[32,2,16,256]{3,2,1,0:T(8,128)(2,1)}), bf16[32,2,16,256]{3,2,1,0:T(8,128)(2,1)S(1)}, u32[]{:S(2)}, u32[]{:S(2)}) %all-to-all-start) | async-done | bytes 524320 | tf_op jit(solution)/shard_map/all_to_all | solution.py:88
  48.4 8.1 %all-to-all-start.1 = ((bf16[32,2,2,32,256]{4,3,2,1,0:T(8,128)(2,1)}), bf16[32,2,2,32,256]{4,3,2,1,0:T(8,128)(2,1)}, u32[]{:S(2)}, u32[]{:S(2)}) async-start(bf16[32,2,2,32,256]{4,3,2,1,0:T(8,128)(2,1)} %scatter_fusion.1), calls=%async_computation.1 | async-start | bytes 4194304 | tf_op jit(solution)/shard_map/all_to_all | solution.py:87
  58.2 4.5 %scatter_custom_fusion.1 = s32[32]{0:T(128)S(1)} fusion(s32[1024]{0:T(1024)S(1)} %bitcast.214, s32[1024]{0:T(1024)S(1)} %reshape.369, s32[]{:T(128)} %constant.117.clone.1), kind=kCustom, calls=%fused_computation.95 | custom fusion | bytes 132 | tf_op jit(solution)/shard_map/scatter | solution.py:92
  64.5 49.6 %all-to-all-done.1 = bf16[32,2,2,32,256]{4,3,2,1,0:T(8,128)(2,1)} async-done(((bf16[32,2,2,32,256]{4,3,2,1,0:T(8,128)(2,1)}), bf16[32,2,2,32,256]{4,3,2,1,0:T(8,128)(2,1)}, u32[]{:S(2)}, u32[]{:S(2)}) %all-to-all-start.1) | async-done | bytes 2097184 | tf_op jit(solution)/shard_map/all_to_all | solution.py:87
  114.1 3.2 %gather_fusion.1 = bf16[32,2,32,256]{3,2,1,0:T(8,128)(2,1)} fusion(bf16[64,2,32,256]{3,2,1,0:T(8,128)(2,1)} %bitcast.17, s32[1024]{0:T(1024)S(1)} %pad_clamp_fusion), kind=kCustom, calls=%fused_computation.1 | custom fusion | bytes 2097280 | tf_op jit(solution)/shard_map/gather | solution.py:93
  117.3 1.3 copy.80
  118.6 1.1 pad_maximum_fusion
  119.7 52.2 %while.32 = (s32[]{:T(128)}, f32[32,16,256]{2,1,0:T(8,128)S(1)}, bf16[4,32,16,128]{3,2,1,0:T(8,128)(2,1)}, f32[32,1]{0,1:T(1,128)S(1)}, f32[4,32,128]{2,0,1:T(4,...) while((s32[]{:T(128)}, f32[32,16,256]{2,1,0:T(8,128)S(1)}, ...), condition=%wide.region_6.7_spmd.clone, body=%wide.region_4.6_spmd.clone.sunk | while | flops 524115968 | bytes 31068848 | solution.py:55
  121.0 1.7 fusion.87
  124.6 3.1 %fusion.88 = bf16[4,32,16,128]{3,2,1,0:T(8,128)(2,1)S(1)} fusion(bf16[4,32,16,128]{3,2,1,0:T(8,128)(2,1)S(1)} %copy-done.8, s32[]{:T(128)} %get-tuple-element.550, f32[32,16,128]{2,1,0:T(8,128)S(1)} %fusion.87, f32[32,256,128]{2,1,0:T(8,128)S(1)} %bitcast.192, f32[32,16,256]{2,1,0:T(8,128)S(1)} %get-tuple-element.551, f32[32]{0:T(128)} %get-tuple-element.569, ...), kind=kOutput, calls=%fused_computation.42.clone.1 | convolution fusion | flops 201654272 | bytes 5390468 | tf_op jit(solution)/shard_map/while/body/eval_jaxpr/hpn,hnt->hpt/dot_general | solution.py:44
  129.2 3.6 %convolution_add_fusion.2 = f32[32,16,256]{2,1,0:T(8,128)S(1)} fusion(f32[32,256,128]{2,1,0:T(8,128)S(1)} %bitcast.193, f32[32,16,256]{2,1,0:T(8,128)S(1)} %get-tuple-element.551, f32[32]{0:T(128)S(1)} %exp.74, f32[32,128]{1,0:T(8,128)S(1)} %get-tuple-element.520, bf16[4,32,16,128]{3,2,1,0:T(8,128)(2,1)S(1)} %get-tuple-element.566, ...), kind=kOutput, calls=%fused_computation.36.clone.1 | convolution fusion | flops 201719808 | bytes 5390852 | tf_op jit(solution)/shard_map/while/body/eval_jaxpr/hps,hns->hpn/dot_general | solution.py:50
  134.0 1.7 fusion.87
  137.7 3.1 %fusion.88 = bf16[4,32,16,128]{3,2,1,0:T(8,128)(2,1)S(1)} fusion(bf16[4,32,16,128]{3,2,1,0:T(8,128)(2,1)S(1)} %copy-done.8, s32[]{:T(128)} %get-tuple-element.550, f32[32,16,128]{2,1,0:T(8,128)S(1)} %fusion.87, f32[32,256,128]{2,1,0:T(8,128)S(1)} %bitcast.192, f32[32,16,256]{2,1,0:T(8,128)S(1)} %get-tuple-element.551, f32[32]{0:T(128)} %get-tuple-element.569, ...), kind=kOutput, calls=%fused_computation.42.clone.1 | convolution fusion | flops 201654272 | bytes 5390468 | tf_op jit(solution)/shard_map/while/body/eval_jaxpr/hpn,hnt->hpt/dot_general | solution.py:44
  142.2 3.6 %convolution_add_fusion.2 = f32[32,16,256]{2,1,0:T(8,128)S(1)} fusion(f32[32,256,128]{2,1,0:T(8,128)S(1)} %bitcast.193, f32[32,16,256]{2,1,0:T(8,128)S(1)} %get-tuple-element.551, f32[32]{0:T(128)S(1)} %exp.74, f32[32,128]{1,0:T(8,128)S(1)} %get-tuple-element.520, bf16[4,32,16,128]{3,2,1,0:T(8,128)(2,1)S(1)} %get-tuple-element.566, ...), kind=kOutput, calls=%fused_computation.36.clone.1 | convolution fusion | flops 201719808 | bytes 5390852 | tf_op jit(solution)/shard_map/while/body/eval_jaxpr/hps,hns->hpn/dot_general | solution.py:50
  147.1 1.7 fusion.87
  150.7 3.1 %fusion.88 = bf16[4,32,16,128]{3,2,1,0:T(8,128)(2,1)S(1)} fusion(bf16[4,32,16,128]{3,2,1,0:T(8,128)(2,1)S(1)} %copy-done.8, s32[]{:T(128)} %get-tuple-element.550, f32[32,16,128]{2,1,0:T(8,128)S(1)} %fusion.87, f32[32,256,128]{2,1,0:T(8,128)S(1)} %bitcast.192, f32[32,16,256]{2,1,0:T(8,128)S(1)} %get-tuple-element.551, f32[32]{0:T(128)} %get-tuple-element.569, ...), kind=kOutput, calls=%fused_computation.42.clone.1 | convolution fusion | flops 201654272 | bytes 5390468 | tf_op jit(solution)/shard_map/while/body/eval_jaxpr/hpn,hnt->hpt/dot_general | solution.py:44
  155.2 3.6 %convolution_add_fusion.2 = f32[32,16,256]{2,1,0:T(8,128)S(1)} fusion(f32[32,256,128]{2,1,0:T(8,128)S(1)} %bitcast.193, f32[32,16,256]{2,1,0:T(8,128)S(1)} %get-tuple-element.551, f32[32]{0:T(128)S(1)} %exp.74, f32[32,128]{1,0:T(8,128)S(1)} %get-tuple-element.520, bf16[4,32,16,128]{3,2,1,0:T(8,128)(2,1)S(1)} %get-tuple-element.566, ...), kind=kOutput, calls=%fused_computation.36.clone.1 | convolution fusion | flops 201719808 | bytes 5390852 | tf_op jit(solution)/shard_map/while/body/eval_jaxpr/hps,hns->hpn/dot_general | solution.py:50
  160.1 1.7 fusion.87
  163.8 3.1 %fusion.88 = bf16[4,32,16,128]{3,2,1,0:T(8,128)(2,1)S(1)} fusion(bf16[4,32,16,128]{3,2,1,0:T(8,128)(2,1)S(1)} %copy-done.8, s32[]{:T(128)} %get-tuple-element.550, f32[32,16,128]{2,1,0:T(8,128)S(1)} %fusion.87, f32[32,256,128]{2,1,0:T(8,128)S(1)} %bitcast.192, f32[32,16,256]{2,1,0:T(8,128)S(1)} %get-tuple-element.551, f32[32]{0:T(128)} %get-tuple-element.569, ...), kind=kOutput, calls=%fused_computation.42.clone.1 | convolution fusion | flops 201654272 | bytes 5390468 | tf_op jit(solution)/shard_map/while/body/eval_jaxpr/hpn,hnt->hpt/dot_general | solution.py:44
  168.3 3.6 %convolution_add_fusion.2 = f32[32,16,256]{2,1,0:T(8,128)S(1)} fusion(f32[32,256,128]{2,1,0:T(8,128)S(1)} %bitcast.193, f32[32,16,256]{2,1,0:T(8,128)S(1)} %get-tuple-element.551, f32[32]{0:T(128)S(1)} %exp.74, f32[32,128]{1,0:T(8,128)S(1)} %get-tuple-element.520, bf16[4,32,16,128]{3,2,1,0:T(8,128)(2,1)S(1)} %get-tuple-element.566, ...), kind=kOutput, calls=%fused_computation.36.clone.1 | convolution fusion | flops 201719808 | bytes 5390852 | tf_op jit(solution)/shard_map/while/body/eval_jaxpr/hps,hns->hpn/dot_general | solution.py:50
  171.9 1.6 copy.79
  173.8 1.6 select_convert_fusion.1
  175.4 7.0 %all-gather.2.cloned.1.call-done = bf16[2,4608,256]{2,1,0:T(8,128)(2,1)} async-done(((bf16[2,1152,256]{2,1,0:T(8,128)(2,1)}), bf16[2,4608,256]{2,1,0:T(8,128)(2,1)}) %all-gather.2.cloned.1.call-update) | async-done | bytes 4718608 | tf_op jit(solution)/shard_map/all_gather | solution.py:154
  182.4 94.4 %while.33 = (s32[]{:T(128)}, f32[128,2,8]{0,2,1:T(8,128)S(1)}, f32[128,2,8]{0,2,1:T(8,128)S(1)}, f32[128,2,8,128]{0,3,2,1:T(8,128)}, s32[4]{0:T(128)S(1)}, /*ind...) while((s32[]{:T(128)}, f32[128,2,8]{0,2,1:T(8,128)S(1)}, ...), condition=%wide.region_11.12_spmd.clone, body=%wide.region_8.11_spmd.clone.sunk | while | flops 1235016192 | bytes 47004440 | solution.py:165
  185.2 1.1 compare_select_fusion.7
  186.2 1.3 constant_dynamic-slice_fusion.10
  188.0 5.3 %fusion.92 = (f32[128,2,8]{0,2,1:T(8,128)S(1)}, f32[2,1152,128,8]{2,1,3,0:T(8,128)}) fusion(pred[128,1152]{0,1:T(8,128)(4,1)S(1)} %compare_select_fusion.7, bf16[1152,2,128,1]{0,2,3,1:T(8,128)(2,1)S(1)} %bitcast.196, bf16[128,2,8,128]{3,2,1,0:T(8,128)(2,1)S(1)} %bitcast.194), kind=kOutput, calls=%fused_computation.9.clone.1 | convolution fusion | flops 611055616 | bytes 10706944 | tf_op jit(solution)/shard_map/while/body/eval_jaxpr/rgqd,kgd->rgqk/dot_general | solution.py:121
  193.3 5.6 %fusion.93 = f32[128,2,8]{0,2,1:T(8,128)S(1)} fusion(f32[2,1152,128,8]{2,1,3,0:T(8,128)} %get-tuple-element.535, f32[128,2,8]{0,2,1:T(8,128)S(1)} %select_maximum_fusion.2, pred[128,1152]{0,1:T(8,128)(4,1)S(1)} %compare_select_fusion.7), kind=kLoop, calls=%fused_computation.13.clone.1 | loop fusion | flops 9435136 | bytes 9601024 | tf_op jit(solution)/shard_map/while/body/eval_jaxpr/reduce_sum | solution.py:128
  199.2 5.9 %fusion.95 = f32[128,2,8,128]{0,3,2,1:T(8,128)S(1)} fusion(bf16[1152,2,128,1]{0,2,3,1:T(8,128)(2,1)S(1)} %bitcast.197, f32[2,1152,128,8]{2,1,3,0:T(8,128)} %get-tuple-element.535, f32[128,2,8]{0,2,1:T(8,128)S(1)} %select_maximum_fusion.2, pred[128,1152]{0,1:T(8,128)(4,1)S(1)} %compare_select_fusion.7, f32[128,2,8,128]{0,3,2,1:T(8,128)S(1)} %copy-done.3, ...), kind=kOutput, calls=%fused_computation.17.clone.1 | convolution fusion | flops 614203392 | bytes 12288001 | tf_op jit(solution)/shard_map/while/body/eval_jaxpr/rgqk,kgd->rgqd/dot_general | solution.py:129
  208.7 1.1 compare_select_fusion.7
  209.8 1.3 constant_dynamic-slice_fusion.10
  211.5 5.3 %fusion.92 = (f32[128,2,8]{0,2,1:T(8,128)S(1)}, f32[2,1152,128,8]{2,1,3,0:T(8,128)}) fusion(pred[128,1152]{0,1:T(8,128)(4,1)S(1)} %compare_select_fusion.7, bf16[1152,2,128,1]{0,2,3,1:T(8,128)(2,1)S(1)} %bitcast.196, bf16[128,2,8,128]{3,2,1,0:T(8,128)(2,1)S(1)} %bitcast.194), kind=kOutput, calls=%fused_computation.9.clone.1 | convolution fusion | flops 611055616 | bytes 10706944 | tf_op jit(solution)/shard_map/while/body/eval_jaxpr/rgqd,kgd->rgqk/dot_general | solution.py:121
  216.8 5.6 %fusion.93 = f32[128,2,8]{0,2,1:T(8,128)S(1)} fusion(f32[2,1152,128,8]{2,1,3,0:T(8,128)} %get-tuple-element.535, f32[128,2,8]{0,2,1:T(8,128)S(1)} %select_maximum_fusion.2, pred[128,1152]{0,1:T(8,128)(4,1)S(1)} %compare_select_fusion.7), kind=kLoop, calls=%fused_computation.13.clone.1 | loop fusion | flops 9435136 | bytes 9601024 | tf_op jit(solution)/shard_map/while/body/eval_jaxpr/reduce_sum | solution.py:128
  222.8 5.9 %fusion.95 = f32[128,2,8,128]{0,3,2,1:T(8,128)S(1)} fusion(bf16[1152,2,128,1]{0,2,3,1:T(8,128)(2,1)S(1)} %bitcast.197, f32[2,1152,128,8]{2,1,3,0:T(8,128)} %get-tuple-element.535, f32[128,2,8]{0,2,1:T(8,128)S(1)} %select_maximum_fusion.2, pred[128,1152]{0,1:T(8,128)(4,1)S(1)} %compare_select_fusion.7, f32[128,2,8,128]{0,3,2,1:T(8,128)S(1)} %copy-done.3, ...), kind=kOutput, calls=%fused_computation.17.clone.1 | convolution fusion | flops 614203392 | bytes 12288001 | tf_op jit(solution)/shard_map/while/body/eval_jaxpr/rgqk,kgd->rgqd/dot_general | solution.py:129
  233.3 1.3 constant_dynamic-slice_fusion.10
  235.0 5.3 %fusion.92 = (f32[128,2,8]{0,2,1:T(8,128)S(1)}, f32[2,1152,128,8]{2,1,3,0:T(8,128)}) fusion(pred[128,1152]{0,1:T(8,128)(4,1)S(1)} %compare_select_fusion.7, bf16[1152,2,128,1]{0,2,3,1:T(8,128)(2,1)S(1)} %bitcast.196, bf16[128,2,8,128]{3,2,1,0:T(8,128)(2,1)S(1)} %bitcast.194), kind=kOutput, calls=%fused_computation.9.clone.1 | convolution fusion | flops 611055616 | bytes 10706944 | tf_op jit(solution)/shard_map/while/body/eval_jaxpr/rgqd,kgd->rgqk/dot_general | solution.py:121
  240.3 5.6 %fusion.93 = f32[128,2,8]{0,2,1:T(8,128)S(1)} fusion(f32[2,1152,128,8]{2,1,3,0:T(8,128)} %get-tuple-element.535, f32[128,2,8]{0,2,1:T(8,128)S(1)} %select_maximum_fusion.2, pred[128,1152]{0,1:T(8,128)(4,1)S(1)} %compare_select_fusion.7), kind=kLoop, calls=%fused_computation.13.clone.1 | loop fusion | flops 9435136 | bytes 9601024 | tf_op jit(solution)/shard_map/while/body/eval_jaxpr/reduce_sum | solution.py:128
  246.3 5.9 %fusion.95 = f32[128,2,8,128]{0,3,2,1:T(8,128)S(1)} fusion(bf16[1152,2,128,1]{0,2,3,1:T(8,128)(2,1)S(1)} %bitcast.197, f32[2,1152,128,8]{2,1,3,0:T(8,128)} %get-tuple-element.535, f32[128,2,8]{0,2,1:T(8,128)S(1)} %select_maximum_fusion.2, pred[128,1152]{0,1:T(8,128)(4,1)S(1)} %compare_select_fusion.7, f32[128,2,8,128]{0,3,2,1:T(8,128)S(1)} %copy-done.3, ...), kind=kOutput, calls=%fused_computation.17.clone.1 | convolution fusion | flops 614203392 | bytes 12288001 | tf_op jit(solution)/shard_map/while/body/eval_jaxpr/rgqk,kgd->rgqd/dot_general | solution.py:129
  256.8 1.3 constant_dynamic-slice_fusion.10
  258.6 5.3 %fusion.92 = (f32[128,2,8]{0,2,1:T(8,128)S(1)}, f32[2,1152,128,8]{2,1,3,0:T(8,128)}) fusion(pred[128,1152]{0,1:T(8,128)(4,1)S(1)} %compare_select_fusion.7, bf16[1152,2,128,1]{0,2,3,1:T(8,128)(2,1)S(1)} %bitcast.196, bf16[128,2,8,128]{3,2,1,0:T(8,128)(2,1)S(1)} %bitcast.194), kind=kOutput, calls=%fused_computation.9.clone.1 | convolution fusion | flops 611055616 | bytes 10706944 | tf_op jit(solution)/shard_map/while/body/eval_jaxpr/rgqd,kgd->rgqk/dot_general | solution.py:121
  263.9 5.6 %fusion.93 = f32[128,2,8]{0,2,1:T(8,128)S(1)} fusion(f32[2,1152,128,8]{2,1,3,0:T(8,128)} %get-tuple-element.535, f32[128,2,8]{0,2,1:T(8,128)S(1)} %select_maximum_fusion.2, pred[128,1152]{0,1:T(8,128)(4,1)S(1)} %compare_select_fusion.7), kind=kLoop, calls=%fused_computation.13.clone.1 | loop fusion | flops 9435136 | bytes 9601024 | tf_op jit(solution)/shard_map/while/body/eval_jaxpr/reduce_sum | solution.py:128
  269.8 5.9 %fusion.95 = f32[128,2,8,128]{0,3,2,1:T(8,128)S(1)} fusion(bf16[1152,2,128,1]{0,2,3,1:T(8,128)(2,1)S(1)} %bitcast.197, f32[2,1152,128,8]{2,1,3,0:T(8,128)} %get-tuple-element.535, f32[128,2,8]{0,2,1:T(8,128)S(1)} %select_maximum_fusion.2, pred[128,1152]{0,1:T(8,128)(4,1)S(1)} %compare_select_fusion.7, f32[128,2,8,128]{0,3,2,1:T(8,128)S(1)} %copy-done.3, ...), kind=kOutput, calls=%fused_computation.17.clone.1 | convolution fusion | flops 614203392 | bytes 12288001 | tf_op jit(solution)/shard_map/while/body/eval_jaxpr/rgqk,kgd->rgqd/dot_general | solution.py:129
  276.7 1.3 broadcast_divide_fusion
  (230 shorter events, 38.5 us)
Async XLA Ops:
  7.2 26.5 %copy-start.2 = (bf16[1,32,2,32,256]{4,3,2,1,0:T(8,128)(2,1)S(1)}, bf16[1,32,2,32,256]{4,3,2,1,0:T(8,128)(2,1)}, u32[]{:S(2)}) copy-start(bf16[1,32,2,32,256]{4,3,2,1,0:T(8,128)(2,1)} %param.18) | copy-start | bytes 3145732
  15.6 32.8 %all-to-all-start = ((bf16[32,2,16,256]{3,2,1,0:T(8,128)(2,1)}), bf16[32,2,16,256]{3,2,1,0:T(8,128)(2,1)S(1)}, u32[]{:S(2)}, u32[]{:S(2)}) async-start(bf16[32,2,16,256]{3,2,1,0:T(8,128)(2,1)} %scatter_fusion), calls=%async_computation | async-start | bytes 1048576 | tf_op jit(solution)/shard_map/all_to_all | solution.py:88
  33.7 23.7 %copy-start.11 = (f32[1,32,512]{2,1,0:T(8,128)S(1)}, f32[1,32,512]{2,1,0:T(8,128)}, u32[]{:S(2)}) copy-start(f32[1,32,512]{2,1,0:T(8,128)} %param.27) | copy-start | bytes 196612
  33.7 23.7 %copy-start.5 = (bf16[1,32,16,512]{3,2,1,0:T(8,128)(2,1)S(1)}, bf16[1,32,16,512]{3,2,1,0:T(8,128)(2,1)}, u32[]{:S(2)}) copy-start(bf16[1,32,16,512]{3,2,1,0:T(8,128)(2,1)} %param.24) | copy-start | bytes 1572868
  33.7 24.0 %copy-start.6 = (bf16[1,2,256,512]{3,2,1,0:T(8,128)(2,1)S(1)}, bf16[1,2,256,512]{3,2,1,0:T(8,128)(2,1)}, u32[]{:S(2)}) copy-start(bf16[1,2,256,512]{3,2,1,0:T(8,128)(2,1)} %param.25) | copy-start | bytes 1572868
  38.7 19.2 %copy-start.7 = (bf16[1,2,256,512]{3,2,1,0:T(8,128)(2,1)S(1)}, bf16[1,2,256,512]{3,2,1,0:T(8,128)(2,1)}, u32[]{:S(2)}) copy-start(bf16[1,2,256,512]{3,2,1,0:T(8,128)(2,1)} %param.26) | copy-start | bytes 1572868
  38.7 19.4 %copy-start.14 = (s32[1,1024]{1,0:T(1,128)S(1)}, s32[1,1024]{1,0:T(1,128)}, u32[]{:S(2)}) copy-start(s32[1,1024]{1,0:T(1,128)} %param.20) | copy-start | bytes 12292
  38.7 19.4 %copy-start.17 = (s32[1,1024]{1,0:T(1,128)S(1)}, s32[1,1024]{1,0:T(1,128)}, u32[]{:S(2)}) copy-start(s32[1,1024]{1,0:T(1,128)} %param.21) | copy-start | bytes 12292
  38.7 25.1 %copy-start.19 = (f32[32]{0:T(128)S(1)}, f32[32]{0:T(128)}, u32[]{:S(2)}) copy-start(f32[32]{0:T(128)} %param.28) | copy-start | bytes 388
  48.4 65.7 %all-to-all-start.1 = ((bf16[32,2,2,32,256]{4,3,2,1,0:T(8,128)(2,1)}), bf16[32,2,2,32,256]{4,3,2,1,0:T(8,128)(2,1)}, u32[]{:S(2)}, u32[]{:S(2)}) async-start(bf16[32,2,2,32,256]{4,3,2,1,0:T(8,128)(2,1)} %scatter_fusion.1), calls=%async_computation.1 | async-start | bytes 4194304 | tf_op jit(solution)/shard_map/all_to_all | solution.py:87
  56.5 125.9 %all-gather.2.cloned.1.call-start = ((), (), s32[]{:S(2)}) async-start(), calls=%async_computation.2 | async-start | bytes 5898240 | tf_op jit(solution)/shard_map/all_gather | solution.py:154
  57.6 61.0 %copy-start.10 = (bf16[1,2,128,256]{3,2,1,0:T(8,128)(2,1)S(1)}, bf16[1,2,128,256]{3,2,1,0:T(8,128)(2,1)}, u32[]{:S(2)}) copy-start(bf16[1,2,128,256]{3,2,1,0:T(8,128)(2,1)} %param.31) | copy-start | bytes 393220
  119.7 62.6 %copy-start.1 = (bf16[1,128,2048]{2,1,0:T(8,128)(2,1)S(1)}, bf16[1,128,2048]{2,1,0:T(8,128)(2,1)}, u32[]{:S(2)}) copy-start(bf16[1,128,2048]{2,1,0:T(8,128)(2,1)} %param.30) | copy-start | bytes 1572868
  119.8 3.3 %copy-start.15 = (f32[32,1]{0,1:T(1,128)}, f32[32,1]{0,1:T(1,128)S(1)}, u32[]{:S(2)}) copy-start(f32[32,1]{0,1:T(1,128)S(1)} %get-tuple-element.564) | copy-start | bytes 388 | tf_op jit(solution)/shard_map/while
  122.9 0.5 copy-start.12
  123.6 1.0 copy-start.8
  123.6 4.1 %copy-start.13 = (f32[32]{0:T(128)S(1)}, f32[32]{0:T(128)}, u32[]{:S(2)}) copy-start(f32[32]{0:T(128)} %copy-done.12) | copy-start | bytes 388 | tf_op jit(solution)/shard_map/while
  127.7 0.8 copy-start.9
  128.7 4.1 %copy-start.16 = (f32[32,1]{0,1:T(1,128)S(1)}, f32[32,1]{0,1:T(1,128)}, u32[]{:S(2)}) copy-start(f32[32,1]{0,1:T(1,128)} %copy-done.15) | copy-start | bytes 388 | tf_op jit(solution)/shard_map/while
  132.8 3.2 %copy-start.15 = (f32[32,1]{0,1:T(1,128)}, f32[32,1]{0,1:T(1,128)S(1)}, u32[]{:S(2)}) copy-start(f32[32,1]{0,1:T(1,128)S(1)} %get-tuple-element.564) | copy-start | bytes 388 | tf_op jit(solution)/shard_map/while
  136.0 0.5 copy-start.12
  136.6 1.0 copy-start.8
  136.6 4.1 %copy-start.13 = (f32[32]{0:T(128)S(1)}, f32[32]{0:T(128)}, u32[]{:S(2)}) copy-start(f32[32]{0:T(128)} %copy-done.12) | copy-start | bytes 388 | tf_op jit(solution)/shard_map/while
  140.8 0.8 copy-start.9
  141.7 4.1 %copy-start.16 = (f32[32,1]{0,1:T(1,128)S(1)}, f32[32,1]{0,1:T(1,128)}, u32[]{:S(2)}) copy-start(f32[32,1]{0,1:T(1,128)} %copy-done.15) | copy-start | bytes 388 | tf_op jit(solution)/shard_map/while
  145.8 3.3 %copy-start.15 = (f32[32,1]{0,1:T(1,128)}, f32[32,1]{0,1:T(1,128)S(1)}, u32[]{:S(2)}) copy-start(f32[32,1]{0,1:T(1,128)S(1)} %get-tuple-element.564) | copy-start | bytes 388 | tf_op jit(solution)/shard_map/while
  149.0 0.5 copy-start.12
  149.7 1.0 copy-start.8
  149.7 4.1 %copy-start.13 = (f32[32]{0:T(128)S(1)}, f32[32]{0:T(128)}, u32[]{:S(2)}) copy-start(f32[32]{0:T(128)} %copy-done.12) | copy-start | bytes 388 | tf_op jit(solution)/shard_map/while
  153.8 0.8 copy-start.9
  154.8 4.1 %copy-start.16 = (f32[32,1]{0,1:T(1,128)S(1)}, f32[32,1]{0,1:T(1,128)}, u32[]{:S(2)}) copy-start(f32[32,1]{0,1:T(1,128)} %copy-done.15) | copy-start | bytes 388 | tf_op jit(solution)/shard_map/while
  158.9 3.3 %copy-start.15 = (f32[32,1]{0,1:T(1,128)}, f32[32,1]{0,1:T(1,128)S(1)}, u32[]{:S(2)}) copy-start(f32[32,1]{0,1:T(1,128)S(1)} %get-tuple-element.564) | copy-start | bytes 388 | tf_op jit(solution)/shard_map/while
  162.0 0.5 copy-start.12
  162.7 1.0 copy-start.8
  162.7 4.1 %copy-start.13 = (f32[32]{0:T(128)S(1)}, f32[32]{0:T(128)}, u32[]{:S(2)}) copy-start(f32[32]{0:T(128)} %copy-done.12) | copy-start | bytes 388 | tf_op jit(solution)/shard_map/while
  166.8 0.8 copy-start.9
  167.8 4.1 %copy-start.16 = (f32[32,1]{0,1:T(1,128)S(1)}, f32[32,1]{0,1:T(1,128)}, u32[]{:S(2)}) copy-start(f32[32,1]{0,1:T(1,128)} %copy-done.15) | copy-start | bytes 388 | tf_op jit(solution)/shard_map/while
  171.9 10.5 %copy-start = (f32[32,16,256]{2,1,0:T(8,128)}, f32[32,16,256]{2,1,0:T(8,128)S(1)}, u32[]{:S(2)}) copy-start(f32[32,16,256]{2,1,0:T(8,128)S(1)} %get-tuple-element.235) | copy-start | bytes 1572868
  182.4 95.9 %copy-start.18 = (pred[128]{0:T(512)(128)(4,1)S(1)}, pred[128]{0:T(512)(128)(4,1)}, u32[]{:S(2)}) copy-start(pred[128]{0:T(512)(128)(4,1)} %add_compare_fusion.1) | copy-start | bytes 388
  193.3 6.0 %copy-start.3 = (f32[128,2,8,128]{0,3,2,1:T(8,128)S(1)}, f32[128,2,8,128]{0,3,2,1:T(8,128)}, u32[]{:S(2)}) copy-start(f32[128,2,8,128]{0,3,2,1:T(8,128)} %get-tuple-element.589) | copy-start | bytes 3145732 | tf_op jit(solution)/shard_map/while
  205.2 1.0 copy-start.4
  216.8 6.0 %copy-start.3 = (f32[128,2,8,128]{0,3,2,1:T(8,128)S(1)}, f32[128,2,8,128]{0,3,2,1:T(8,128)}, u32[]{:S(2)}) copy-start(f32[128,2,8,128]{0,3,2,1:T(8,128)} %get-tuple-element.589) | copy-start | bytes 3145732 | tf_op jit(solution)/shard_map/while
  228.7 1.0 copy-start.4
  240.3 6.0 %copy-start.3 = (f32[128,2,8,128]{0,3,2,1:T(8,128)S(1)}, f32[128,2,8,128]{0,3,2,1:T(8,128)}, u32[]{:S(2)}) copy-start(f32[128,2,8,128]{0,3,2,1:T(8,128)} %get-tuple-element.589) | copy-start | bytes 3145732 | tf_op jit(solution)/shard_map/while
  252.2 1.0 copy-start.4
  263.8 6.0 %copy-start.3 = (f32[128,2,8,128]{0,3,2,1:T(8,128)S(1)}, f32[128,2,8,128]{0,3,2,1:T(8,128)}, u32[]{:S(2)}) copy-start(f32[128,2,8,128]{0,3,2,1:T(8,128)} %get-tuple-element.589) | copy-start | bytes 3145732 | tf_op jit(solution)/shard_map/while
  275.7 1.0 copy-start.4
Sparse Core Ops, SparseCore 0:
  119.8 62.4 all-gather.1
where the time goes:
time: 287 us; the launch traced here: 286 us
  matrix products  79.2 us (28%)
  waiting for transfers between devices  66.3 us (23%)
  local copies, waits for them, and re-layouts  51.9 us (18%)
  other arithmetic  42.7 us (15%)
  starting transfers between devices  24.6 us (9%)
  between operations  15 us (5%)
  loops' own time  6.46 us (2%)
    all_to_all x1, waiting for transfers between devices, route_blocks(): lax.all_to_all(send_kv, 'pool', split_axis=0, concat_axis=0, tiled=True)  49.6 us
    dot_general x4, matrix products, attend_block(): jnp.einsum('rgqk,kgd->rgqd', weights.astype(jnp.bfloat16), value_heads, p...  23.6 us
    reduce_sum x4, other arithmetic, attend_block(): totals = fade * totals + jnp.sum(weights, axis=-1)  22.6 us
    dot_general x4, matrix products, attend_block(): jnp.einsum('rgqd,kgd->rgqk', query_heads, key_heads, preferred_element_ty...  21.1 us
    all_to_all x1, starting transfers between devices, route_blocks(): lax.all_to_all(send_state, 'pool', split_axis=0, concat_axis=0, tiled=True)  16.5 us
    dot_general x4, matrix products, advance(): jnp.einsum('hps,hns->hpn', value_blk * weights[:, None, :], write_in, pre...  14.5 us
    while x80, local copies, waits for them, and re-layouts  13.7 us
    dot_general x4, matrix products, advance(): jnp.einsum('hpn,hnt->hpt', carried, read_out, precision=exact)  12.3 us
  transfers between devices with their start and end apart: 3, of which 3 were waited for; matrix products, arithmetic and copies ran while one was open for 21% of the time, Pallas kernels for 0%

commit v1 on v0

--- a/solution.py
+++ b/solution.py
@@ -151,7 +151,8 @@
         jnp.zeros((turn_rows, groups, per_group), jnp.float32),
         jnp.zeros((turn_rows, groups, per_group, HEAD_DIM), jnp.float32),
     )
-    piece = lax.all_gather(local_keys, "ctx", axis=1, tiled=True)
+    outgoing = jnp.stack([local_keys] * lax.axis_size("ctx"))
+    piece = jnp.concatenate(lax.all_to_all(outgoing, "ctx", 0, 0), axis=1)
     count = piece.shape[1] // seg_rows
     blocks = piece.reshape(2, count, seg_rows, width).transpose(1, 0, 2, 3)
 

time: 287 us -> 266 us (0.927)
  the two profiles are of different devices: /device:TPU:1 before, /device:TPU:160 now
where the time goes in v1:
time: 266 us; the launch traced here: 265 us
  waiting for transfers between devices  69.9 us (26%)
  matrix products  68.7 us (26%)
  local copies, waits for them, and re-layouts  49.6 us (19%)
  other arithmetic  40.1 us (15%)
  starting transfers between devices  28.7 us (11%)
  loops' own time  6.12 us (2%)
    all_to_all x1, waiting for transfers between devices, route_blocks(): lax.all_to_all(send_kv, 'pool', split_axis=0, concat_axis=0, tiled=True)  57 us
    reduce_sum x4, other arithmetic, attend_block(): totals = fade * totals + jnp.sum(weights, axis=-1)  22.8 us
    dot_general x4, matrix products, attend_block(): jnp.einsum('rgqd,kgd->rgqk', query_heads, key_heads, preferred_element_ty...  21.1 us
    dot_general x4, matrix products, attend_block(): jnp.einsum('rgqk,kgd->rgqd', weights.astype(jnp.bfloat16), value_heads, p...  15.8 us
    dot_general x4, matrix products, advance(): jnp.einsum('hps,hns->hpn', value_blk * weights[:, None, :], write_in, pre...  14.5 us
    all_to_all x1, starting transfers between devices, route_blocks(): lax.all_to_all(send_state, 'pool', split_axis=0, concat_axis=0, tiled=True)  14 us
    dot_general x4, matrix products, advance(): jnp.einsum('hpn,hnt->hpt', carried, read_out, precision=exact)  9.66 us
    all_to_all x1, starting transfers between devices, route_blocks(): lax.all_to_all(send_kv, 'pool', split_axis=0, concat_axis=0, tiled=True)  9.46 us
  transfers between devices with their start and end apart: 3, of which 3 were waited for; matrix products, arithmetic and copies ran while one was open for 21% of the time, Pallas kernels for 0%

profile of v1, /device:TPU:160, one launch (start us, length us, event | category | flops | bytes accessed | tf_op | source)
XLA Modules:
  0.0 264.8 jit_solution(3307555441109738215)
XLA Ops:
  1.2 1.3 reduce.7
  4.8 4.3 %scatter_fusion = bf16[32,2,16,256]{3,2,1,0:T(8,128)(2,1)} fusion(bf16[32,2,16,256]{3,2,1,0:T(8,128)(2,1)} %broadcast_in_dim.176, s32[32]{0:T(128)S(1)} %fusion.47, bf16[32,16,256]{2,1,0:T(8,128)(2,1)} %param.19), kind=kCustom, calls=%fused_computation.2 | custom fusion | bytes 786688 | tf_op jit(solution)/shard_map/scatter | solution.py:84
  9.1 14.0 %all-to-all-start = ((bf16[32,2,16,256]{3,2,1,0:T(8,128)(2,1)}), bf16[32,2,16,256]{3,2,1,0:T(8,128)(2,1)S(1)}, u32[]{:S(2)}, u32[]{:S(2)}) async-start(bf16[32,2,16,256]{3,2,1,0:T(8,128)(2,1)} %scatter_fusion), calls=%async_computation | async-start | bytes 1048576 | tf_op jit(solution)/shard_map/all_to_all | solution.py:88
  23.1 1.6 broadcast_in_dim.189
  24.7 4.9 %scatter_fusion.1 = bf16[32,2,2,32,256]{4,3,2,1,0:T(8,128)(2,1)} fusion(bf16[32,2,2,32,256]{4,3,2,1,0:T(8,128)(2,1)} %broadcast_in_dim.189, s32[32]{0:T(128)S(1)} %fusion.47, bf16[32,2,32,256]{3,2,1,0:T(8,128)(2,1)S(1)} %bitcast.206), kind=kCustom, calls=%fused_computation.4 | custom fusion | bytes 3145984 | tf_op jit(solution)/shard_map/scatter | solution.py:79
  29.6 8.7 %all-to-all-done = bf16[32,2,16,256]{3,2,1,0:T(8,128)(2,1)S(1)} async-done(((bf16[32,2,16,256]{3,2,1,0:T(8,128)(2,1)}), bf16[32,2,16,256]{3,2,1,0:T(8,128)(2,1)S(1)}, u32[]{:S(2)}, u32[]{:S(2)}) %all-to-all-start) | async-done | bytes 524320 | tf_op jit(solution)/shard_map/all_to_all | solution.py:88
  38.3 9.5 %all-to-all-start.1 = ((bf16[32,2,2,32,256]{4,3,2,1,0:T(8,128)(2,1)}), bf16[32,2,2,32,256]{4,3,2,1,0:T(8,128)(2,1)}, u32[]{:S(2)}, u32[]{:S(2)}) async-start(bf16[32,2,2,32,256]{4,3,2,1,0:T(8,128)(2,1)} %scatter_fusion.1), calls=%async_computation.1 | async-start | bytes 4194304 | tf_op jit(solution)/shard_map/all_to_all | solution.py:87
  49.4 4.3 %scatter_custom_fusion.1 = s32[32]{0:T(128)S(1)} fusion(s32[1024]{0:T(1024)S(1)} %bitcast.210, s32[1024]{0:T(1024)S(1)} %reshape.367, s32[]{:T(128)} %constant.117.clone.1), kind=kCustom, calls=%fused_computation.95 | custom fusion | bytes 132 | tf_op jit(solution)/shard_map/scatter | solution.py:92
  54.4 57.0 %all-to-all-done.1 = bf16[32,2,2,32,256]{4,3,2,1,0:T(8,128)(2,1)} async-done(((bf16[32,2,2,32,256]{4,3,2,1,0:T(8,128)(2,1)}), bf16[32,2,2,32,256]{4,3,2,1,0:T(8,128)(2,1)}, u32[]{:S(2)}, u32[]{:S(2)}) %all-to-all-start.1) | async-done | bytes 2097184 | tf_op jit(solution)/shard_map/all_to_all | solution.py:87
  111.5 2.2 gather_fusion.1
  113.9 1.4 copy.68
  115.3 4.0 %stack.2 = bf16[4,2,1152,256]{2,3,1,0:T(8,128)(2,1)} broadcast(bf16[2,1152,256]{1,2,0:T(8,128)(2,1)} %copy.68), dimensions={1,2,3} | broadcast | bytes 5898240 | tf_op jit(solution)/shard_map/stack | solution.py:154
  119.3 5.2 %all-to-all-start.2 = ((bf16[4,2,1152,256]{2,3,1,0:T(8,128)(2,1)}), bf16[4,2,1152,256]{2,3,1,0:T(8,128)(2,1)}, u32[]{:S(2)}, u32[]{:S(2)}) async-start(bf16[4,2,1152,256]{2,3,1,0:T(8,128)(2,1)} %stack.2), calls=%async_computation.2 | async-start | bytes 9437184 | tf_op jit(solution)/shard_map/all_to_all | solution.py:155
  124.6 47.7 %while.32 = (s32[]{:T(128)}, f32[32,16,256]{2,1,0:T(8,128)S(1)}, bf16[4,32,16,128]{3,2,1,0:T(8,128)(2,1)}, f32[32,1]{0,1:T(1,128)S(1)}, f32[4,32,128]{2,0,1:T(4,...) while((s32[]{:T(128)}, f32[32,16,256]{2,1,0:T(8,128)S(1)}, ...), condition=%wide.region_6.7_spmd.clone, body=%wide.region_4.6_spmd.clone.sunk | while | flops 524115968 | bytes 31067072 | solution.py:55
  125.8 1.7 fusion.87
  129.0 2.4 fusion.88
  132.9 3.6 %convolution_add_fusion.2 = f32[32,16,256]{2,1,0:T(8,128)S(1)} fusion(f32[32,256,128]{2,1,0:T(8,128)S(1)} %bitcast.190, f32[32,16,256]{2,1,0:T(8,128)S(1)} %get-tuple-element.506, f32[32]{0:T(128)S(1)} %exp.74, f32[32,128]{1,0:T(8,128)S(1)} %get-tuple-element.475, bf16[4,32,16,128]{3,2,1,0:T(8,128)(2,1)S(1)} %get-tuple-element.521, ...), kind=kOutput, calls=%fused_computation.36.clone.1 | convolution fusion | flops 201719808 | bytes 5390852 | tf_op jit(solution)/shard_map/while/body/eval_jaxpr/hps,hns->hpn/dot_general | solution.py:50
  137.7 1.7 fusion.87
  140.9 2.4 fusion.88
  144.8 3.6 %convolution_add_fusion.2 = f32[32,16,256]{2,1,0:T(8,128)S(1)} fusion(f32[32,256,128]{2,1,0:T(8,128)S(1)} %bitcast.190, f32[32,16,256]{2,1,0:T(8,128)S(1)} %get-tuple-element.506, f32[32]{0:T(128)S(1)} %exp.74, f32[32,128]{1,0:T(8,128)S(1)} %get-tuple-element.475, bf16[4,32,16,128]{3,2,1,0:T(8,128)(2,1)S(1)} %get-tuple-element.521, ...), kind=kOutput, calls=%fused_computation.36.clone.1 | convolution fusion | flops 201719808 | bytes 5390852 | tf_op jit(solution)/shard_map/while/body/eval_jaxpr/hps,hns->hpn/dot_general | solution.py:50
  149.6 1.7 fusion.87
  152.9 2.4 fusion.88
  156.7 3.6 %convolution_add_fusion.2 = f32[32,16,256]{2,1,0:T(8,128)S(1)} fusion(f32[32,256,128]{2,1,0:T(8,128)S(1)} %bitcast.190, f32[32,16,256]{2,1,0:T(8,128)S(1)} %get-tuple-element.506, f32[32]{0:T(128)S(1)} %exp.74, f32[32,128]{1,0:T(8,128)S(1)} %get-tuple-element.475, bf16[4,32,16,128]{3,2,1,0:T(8,128)(2,1)S(1)} %get-tuple-element.521, ...), kind=kOutput, calls=%fused_computation.36.clone.1 | convolution fusion | flops 201719808 | bytes 5390852 | tf_op jit(solution)/shard_map/while/body/eval_jaxpr/hps,hns->hpn/dot_general | solution.py:50
  161.6 1.7 fusion.87
  164.8 2.4 fusion.88
  168.6 3.6 %convolution_add_fusion.2 = f32[32,16,256]{2,1,0:T(8,128)S(1)} fusion(f32[32,256,128]{2,1,0:T(8,128)S(1)} %bitcast.190, f32[32,16,256]{2,1,0:T(8,128)S(1)} %get-tuple-element.506, f32[32]{0:T(128)S(1)} %exp.74, f32[32,128]{1,0:T(8,128)S(1)} %get-tuple-element.475, bf16[4,32,16,128]{3,2,1,0:T(8,128)(2,1)S(1)} %get-tuple-element.521, ...), kind=kOutput, calls=%fused_computation.36.clone.1 | convolution fusion | flops 201719808 | bytes 5390852 | tf_op jit(solution)/shard_map/while/body/eval_jaxpr/hps,hns->hpn/dot_general | solution.py:50
  172.3 1.6 copy.66
  175.0 4.2 %all-to-all-done.2 = bf16[4,2,1152,256]{2,3,1,0:T(8,128)(2,1)} async-done(((bf16[4,2,1152,256]{2,3,1,0:T(8,128)(2,1)}), bf16[4,2,1152,256]{2,3,1,0:T(8,128)(2,1)}, u32[]{:S(2)}, u32[]{:S(2)}) %all-to-all-start.2) | async-done | bytes 4718624 | tf_op jit(solution)/shard_map/all_to_all | solution.py:155
  179.2 83.0 %while.33 = (s32[]{:T(128)}, f32[128,2,8]{0,2,1:T(8,128)S(1)}, f32[128,2,8]{0,2,1:T(8,128)S(1)}, f32[128,2,8,128]{0,3,2,1:T(8,128)}, s32[4]{0:T(128)S(1)}, /*ind...) while((s32[]{:T(128)}, f32[128,2,8]{0,2,1:T(8,128)S(1)}, ...), condition=%wide.region_11.12_spmd.clone, body=%wide.region_8.11_spmd.clone.sunk | while | flops 1235016192 | bytes 74005248 | solution.py:166
  182.0 1.1 compare_select_fusion.7
  183.1 1.3 constant_dynamic-slice_fusion.10
  184.6 5.3 %fusion.92 = (f32[128,2,8]{0,2,1:T(8,128)S(1)}, f32[2,1152,128,8]{2,1,3,0:T(8,128)}) fusion(pred[128,1152]{0,1:T(8,128)(4,1)S(1)} %compare_select_fusion.7, bf16[1152,2,128,1]{0,2,3,1:T(8,128)(2,1)S(1)} %bitcast.193, bf16[128,2,8,128]{3,2,1,0:T(8,128)(2,1)S(1)} %bitcast.191), kind=kOutput, calls=%fused_computation.9.clone.1 | convolution fusion | flops 611055616 | bytes 10706944 | tf_op jit(solution)/shard_map/while/body/eval_jaxpr/rgqd,kgd->rgqk/dot_general | solution.py:121
  189.8 5.7 %fusion.93 = f32[128,2,8]{0,2,1:T(8,128)S(1)} fusion(f32[2,1152,128,8]{2,1,3,0:T(8,128)} %get-tuple-element.490, f32[128,2,8]{0,2,1:T(8,128)S(1)} %select_maximum_fusion.2, pred[128,1152]{0,1:T(8,128)(4,1)S(1)} %compare_select_fusion.7), kind=kLoop, calls=%fused_computation.13.clone.1 | loop fusion | flops 9435136 | bytes 9601024 | tf_op jit(solution)/shard_map/while/body/eval_jaxpr/reduce_sum | solution.py:128
  196.2 3.0 %fusion.95 = f32[128,2,8,128]{0,3,2,1:T(8,128)} fusion(bf16[1152,2,128,1]{0,2,3,1:T(8,128)(2,1)S(1)} %bitcast.194, f32[2,1152,128,8]{2,1,3,0:T(8,128)S(1)} %copy-done, f32[128,2,8]{0,2,1:T(8,128)S(1)} %select_maximum_fusion.2, pred[128,1152]{0,1:T(8,128)(4,1)S(1)} %compare_select_fusion.7, f32[128,2,8,128]{0,3,2,1:T(8,128)} %get-tuple-element.544, ...), kind=kOutput, calls=%fused_computation.17.clone.1 | convolution fusion | flops 614203392 | bytes 12288001 | tf_op jit(solution)/shard_map/while/body/eval_jaxpr/rgqk,kgd->rgqd/dot_general | solution.py:129
  202.9 1.3 constant_dynamic-slice_fusion.10
  204.3 5.3 %fusion.92 = (f32[128,2,8]{0,2,1:T(8,128)S(1)}, f32[2,1152,128,8]{2,1,3,0:T(8,128)}) fusion(pred[128,1152]{0,1:T(8,128)(4,1)S(1)} %compare_select_fusion.7, bf16[1152,2,128,1]{0,2,3,1:T(8,128)(2,1)S(1)} %bitcast.193, bf16[128,2,8,128]{3,2,1,0:T(8,128)(2,1)S(1)} %bitcast.191), kind=kOutput, calls=%fused_computation.9.clone.1 | convolution fusion | flops 611055616 | bytes 10706944 | tf_op jit(solution)/shard_map/while/body/eval_jaxpr/rgqd,kgd->rgqk/dot_general | solution.py:121
  209.6 5.7 %fusion.93 = f32[128,2,8]{0,2,1:T(8,128)S(1)} fusion(f32[2,1152,128,8]{2,1,3,0:T(8,128)} %get-tuple-element.490, f32[128,2,8]{0,2,1:T(8,128)S(1)} %select_maximum_fusion.2, pred[128,1152]{0,1:T(8,128)(4,1)S(1)} %compare_select_fusion.7), kind=kLoop, calls=%fused_computation.13.clone.1 | loop fusion | flops 9435136 | bytes 9601024 | tf_op jit(solution)/shard_map/while/body/eval_jaxpr/reduce_sum | solution.py:128
  216.0 4.3 %fusion.95 = f32[128,2,8,128]{0,3,2,1:T(8,128)} fusion(bf16[1152,2,128,1]{0,2,3,1:T(8,128)(2,1)S(1)} %bitcast.194, f32[2,1152,128,8]{2,1,3,0:T(8,128)S(1)} %copy-done, f32[128,2,8]{0,2,1:T(8,128)S(1)} %select_maximum_fusion.2, pred[128,1152]{0,1:T(8,128)(4,1)S(1)} %compare_select_fusion.7, f32[128,2,8,128]{0,3,2,1:T(8,128)} %get-tuple-element.544, ...), kind=kOutput, calls=%fused_computation.17.clone.1 | convolution fusion | flops 614203392 | bytes 12288001 | tf_op jit(solution)/shard_map/while/body/eval_jaxpr/rgqk,kgd->rgqd/dot_general | solution.py:129
  222.8 1.1 compare_select_fusion.7
  223.9 1.3 constant_dynamic-slice_fusion.10
  225.3 5.3 %fusion.92 = (f32[128,2,8]{0,2,1:T(8,128)S(1)}, f32[2,1152,128,8]{2,1,3,0:T(8,128)}) fusion(pred[128,1152]{0,1:T(8,128)(4,1)S(1)} %compare_select_fusion.7, bf16[1152,2,128,1]{0,2,3,1:T(8,128)(2,1)S(1)} %bitcast.193, bf16[128,2,8,128]{3,2,1,0:T(8,128)(2,1)S(1)} %bitcast.191), kind=kOutput, calls=%fused_computation.9.clone.1 | convolution fusion | flops 611055616 | bytes 10706944 | tf_op jit(solution)/shard_map/while/body/eval_jaxpr/rgqd,kgd->rgqk/dot_general | solution.py:121
  230.6 5.7 %fusion.93 = f32[128,2,8]{0,2,1:T(8,128)S(1)} fusion(f32[2,1152,128,8]{2,1,3,0:T(8,128)} %get-tuple-element.490, f32[128,2,8]{0,2,1:T(8,128)S(1)} %select_maximum_fusion.2, pred[128,1152]{0,1:T(8,128)(4,1)S(1)} %compare_select_fusion.7), kind=kLoop, calls=%fused_computation.13.clone.1 | loop fusion | flops 9435136 | bytes 9601024 | tf_op jit(solution)/shard_map/while/body/eval_jaxpr/reduce_sum | solution.py:128
  237.0 4.3 %fusion.95 = f32[128,2,8,128]{0,3,2,1:T(8,128)} fusion(bf16[1152,2,128,1]{0,2,3,1:T(8,128)(2,1)S(1)} %bitcast.194, f32[2,1152,128,8]{2,1,3,0:T(8,128)S(1)} %copy-done, f32[128,2,8]{0,2,1:T(8,128)S(1)} %select_maximum_fusion.2, pred[128,1152]{0,1:T(8,128)(4,1)S(1)} %compare_select_fusion.7, f32[128,2,8,128]{0,3,2,1:T(8,128)} %get-tuple-element.544, ...), kind=kOutput, calls=%fused_computation.17.clone.1 | convolution fusion | flops 614203392 | bytes 12288001 | tf_op jit(solution)/shard_map/while/body/eval_jaxpr/rgqk,kgd->rgqd/dot_general | solution.py:129
  244.9 1.3 constant_dynamic-slice_fusion.10
  246.3 5.3 %fusion.92 = (f32[128,2,8]{0,2,1:T(8,128)S(1)}, f32[2,1152,128,8]{2,1,3,0:T(8,128)}) fusion(pred[128,1152]{0,1:T(8,128)(4,1)S(1)} %compare_select_fusion.7, bf16[1152,2,128,1]{0,2,3,1:T(8,128)(2,1)S(1)} %bitcast.193, bf16[128,2,8,128]{3,2,1,0:T(8,128)(2,1)S(1)} %bitcast.191), kind=kOutput, calls=%fused_computation.9.clone.1 | convolution fusion | flops 611055616 | bytes 10706944 | tf_op jit(solution)/shard_map/while/body/eval_jaxpr/rgqd,kgd->rgqk/dot_general | solution.py:121
  251.6 5.7 %fusion.93 = f32[128,2,8]{0,2,1:T(8,128)S(1)} fusion(f32[2,1152,128,8]{2,1,3,0:T(8,128)} %get-tuple-element.490, f32[128,2,8]{0,2,1:T(8,128)S(1)} %select_maximum_fusion.2, pred[128,1152]{0,1:T(8,128)(4,1)S(1)} %compare_select_fusion.7), kind=kLoop, calls=%fused_computation.13.clone.1 | loop fusion | flops 9435136 | bytes 9601024 | tf_op jit(solution)/shard_map/while/body/eval_jaxpr/reduce_sum | solution.py:128
  258.0 4.3 %fusion.95 = f32[128,2,8,128]{0,3,2,1:T(8,128)} fusion(bf16[1152,2,128,1]{0,2,3,1:T(8,128)(2,1)S(1)} %bitcast.194, f32[2,1152,128,8]{2,1,3,0:T(8,128)S(1)} %copy-done, f32[128,2,8]{0,2,1:T(8,128)S(1)} %select_maximum_fusion.2, pred[128,1152]{0,1:T(8,128)(4,1)S(1)} %compare_select_fusion.7, f32[128,2,8,128]{0,3,2,1:T(8,128)} %get-tuple-element.544, ...), kind=kOutput, calls=%fused_computation.17.clone.1 | convolution fusion | flops 614203392 | bytes 12288001 | tf_op jit(solution)/shard_map/while/body/eval_jaxpr/rgqk,kgd->rgqd/dot_general | solution.py:129
  262.2 1.3 broadcast_divide_fusion
  (183 shorter events, 33.0 us)
Async XLA Ops:
  0.6 24.0 %copy-start.3 = (bf16[1,32,2,32,256]{4,3,2,1,0:T(8,128)(2,1)S(1)}, bf16[1,32,2,32,256]{4,3,2,1,0:T(8,128)(2,1)}, u32[]{:S(2)}) copy-start(bf16[1,32,2,32,256]{4,3,2,1,0:T(8,128)(2,1)} %param.18) | copy-start | bytes 3145732
  9.1 29.2 %all-to-all-start = ((bf16[32,2,16,256]{3,2,1,0:T(8,128)(2,1)}), bf16[32,2,16,256]{3,2,1,0:T(8,128)(2,1)S(1)}, u32[]{:S(2)}, u32[]{:S(2)}) async-start(bf16[32,2,16,256]{3,2,1,0:T(8,128)(2,1)} %scatter_fusion), calls=%async_computation | async-start | bytes 1048576 | tf_op jit(solution)/shard_map/all_to_all | solution.py:88
  24.7 24.0 %copy-start.10 = (f32[1,32,512]{2,1,0:T(8,128)S(1)}, f32[1,32,512]{2,1,0:T(8,128)}, u32[]{:S(2)}) copy-start(f32[1,32,512]{2,1,0:T(8,128)} %param.27) | copy-start | bytes 196612
  24.7 24.0 %copy-start.4 = (bf16[1,32,16,512]{3,2,1,0:T(8,128)(2,1)S(1)}, bf16[1,32,16,512]{3,2,1,0:T(8,128)(2,1)}, u32[]{:S(2)}) copy-start(bf16[1,32,16,512]{3,2,1,0:T(8,128)(2,1)} %param.24) | copy-start | bytes 1572868
  24.7 24.2 %copy-start.5 = (bf16[1,2,256,512]{3,2,1,0:T(8,128)(2,1)S(1)}, bf16[1,2,256,512]{3,2,1,0:T(8,128)(2,1)}, u32[]{:S(2)}) copy-start(bf16[1,2,256,512]{3,2,1,0:T(8,128)(2,1)} %param.25) | copy-start | bytes 1572868
  29.6 19.5 %copy-start.6 = (bf16[1,2,256,512]{3,2,1,0:T(8,128)(2,1)S(1)}, bf16[1,2,256,512]{3,2,1,0:T(8,128)(2,1)}, u32[]{:S(2)}) copy-start(bf16[1,2,256,512]{3,2,1,0:T(8,128)(2,1)} %param.26) | copy-start | bytes 1572868
  29.6 19.7 %copy-start.11 = (s32[1,1024]{1,0:T(1,128)S(1)}, s32[1,1024]{1,0:T(1,128)}, u32[]{:S(2)}) copy-start(s32[1,1024]{1,0:T(1,128)} %param.20) | copy-start | bytes 12292
  29.6 19.7 %copy-start.13 = (s32[1,1024]{1,0:T(1,128)S(1)}, s32[1,1024]{1,0:T(1,128)}, u32[]{:S(2)}) copy-start(s32[1,1024]{1,0:T(1,128)} %param.21) | copy-start | bytes 12292
  29.6 24.1 %copy-start.14 = (f32[32]{0:T(128)S(1)}, f32[32]{0:T(128)}, u32[]{:S(2)}) copy-start(f32[32]{0:T(128)} %param.28) | copy-start | bytes 388
  38.3 73.2 %all-to-all-start.1 = ((bf16[32,2,2,32,256]{4,3,2,1,0:T(8,128)(2,1)}), bf16[32,2,2,32,256]{4,3,2,1,0:T(8,128)(2,1)}, u32[]{:S(2)}, u32[]{:S(2)}) async-start(bf16[32,2,2,32,256]{4,3,2,1,0:T(8,128)(2,1)} %scatter_fusion.1), calls=%async_computation.1 | async-start | bytes 4194304 | tf_op jit(solution)/shard_map/all_to_all | solution.py:87
  48.8 65.0 %copy-start.9 = (bf16[1,2,128,256]{3,2,1,0:T(8,128)(2,1)S(1)}, bf16[1,2,128,256]{3,2,1,0:T(8,128)(2,1)}, u32[]{:S(2)}) copy-start(bf16[1,2,128,256]{3,2,1,0:T(8,128)(2,1)} %param.31) | copy-start | bytes 393220
  119.3 5.2 %copy-start.12 = (f32[32]{0:T(128)S(1)}, f32[32]{0:T(128)}, u32[]{:S(2)}) copy-start(f32[32]{0:T(128)} %param.29) | copy-start | bytes 388
  119.3 59.9 %all-to-all-start.2 = ((bf16[4,2,1152,256]{2,3,1,0:T(8,128)(2,1)}), bf16[4,2,1152,256]{2,3,1,0:T(8,128)(2,1)}, u32[]{:S(2)}, u32[]{:S(2)}) async-start(bf16[4,2,1152,256]{2,3,1,0:T(8,128)(2,1)} %stack.2), calls=%async_computation.2 | async-start | bytes 9437184 | tf_op jit(solution)/shard_map/all_to_all | solution.py:155
  124.5 54.7 %copy-start.2 = (bf16[1,128,2048]{2,1,0:T(8,128)(2,1)S(1)}, bf16[1,128,2048]{2,1,0:T(8,128)(2,1)}, u32[]{:S(2)}) copy-start(bf16[1,128,2048]{2,1,0:T(8,128)(2,1)} %param.30) | copy-start | bytes 1572868
  128.0 1.0 copy-start.7
  131.4 0.8 copy-start.8
  139.9 1.0 copy-start.7
  143.4 0.8 copy-start.8
  151.8 1.0 copy-start.7
  155.3 0.8 copy-start.8
  163.7 1.0 copy-start.7
  167.2 0.8 copy-start.8
  172.2 7.0 %copy-start.1 = (f32[32,16,256]{2,1,0:T(8,128)}, f32[32,16,256]{2,1,0:T(8,128)S(1)}, u32[]{:S(2)}) copy-start(f32[32,16,256]{2,1,0:T(8,128)S(1)} %get-tuple-element.235) | copy-start | bytes 1572868
  189.8 6.4 %copy-start = (f32[2,1152,128,8]{2,1,3,0:T(8,128)S(1)}, f32[2,1152,128,8]{2,1,3,0:T(8,128)}, u32[]{:S(2)}) copy-start(f32[2,1152,128,8]{2,1,3,0:T(8,128)} %get-tuple-element.490) | copy-start | bytes 28311556 | tf_op jit(solution)/shard_map/while
  209.6 6.4 %copy-start = (f32[2,1152,128,8]{2,1,3,0:T(8,128)S(1)}, f32[2,1152,128,8]{2,1,3,0:T(8,128)}, u32[]{:S(2)}) copy-start(f32[2,1152,128,8]{2,1,3,0:T(8,128)} %get-tuple-element.490) | copy-start | bytes 28311556 | tf_op jit(solution)/shard_map/while
  230.6 6.4 %copy-start = (f32[2,1152,128,8]{2,1,3,0:T(8,128)S(1)}, f32[2,1152,128,8]{2,1,3,0:T(8,128)}, u32[]{:S(2)}) copy-start(f32[2,1152,128,8]{2,1,3,0:T(8,128)} %get-tuple-element.490) | copy-start | bytes 28311556 | tf_op jit(solution)/shard_map/while
  251.6 6.4 %copy-start = (f32[2,1152,128,8]{2,1,3,0:T(8,128)S(1)}, f32[2,1152,128,8]{2,1,3,0:T(8,128)}, u32[]{:S(2)}) copy-start(f32[2,1152,128,8]{2,1,3,0:T(8,128)} %get-tuple-element.490) | copy-start | bytes 28311556 | tf_op jit(solution)/shard_map/while
